TPU v7x, 32 devices: a whole 2x2x4 slice. The times are simulated.
32 devices in a mesh: grp: 4 (over x, core), sec: 8 (over z, y).
Axes of the slice: x: 2, y: 2, z: 4, core: 2. Of those that a mesh axis runs over, the one named last changes fastest.
Arguments:
- trial: bfloat16 [2, 8, 256, 256], P(None, 'sec', 'grp'), may hold values from -6 to 6
- left_ops: bfloat16 [64, 8, 256, 256], P('grp', 'sec'), may hold values from -0.375 to 0.375
- right_ops: bfloat16 [64, 8, 256, 256], P('grp', 'sec'), may hold values from -0.046875 to 0.046875
- source: int32 [64, 8], P('grp', 'sec'), may hold values from 0 to 7
- live: int32 [64, 8], P('grp', 'sec'), may hold values 0 or 1
Outputs:
- sigma: bfloat16 [2, 8, 256, 256], P(None, 'sec', 'grp')
All inputs are finite; a program needn't handle non-finite values. No bound on the sum of `live` on one device may be relied on, other than what follows from the above.
Results may differ from a plain program's by a relative error of at most 0.0049.
Values may be sent and summed in bfloat16 or wider, within the bound.
No kernel may reach another device: no remote copies, remote signals or barrier semaphores. Data moves between devices by JAX's collectives and lax.ppermute only.
A program may use at most 64 MiB of HBM per device.

v0:
```python
import jax
import jax.numpy as jnp
from jax import lax
from jax.sharding import PartitionSpec as P


def body(trial, left_ops, right_ops, source, live):
    own_block = lax.all_gather(trial, "grp", axis=2, tiled=True)
    gathered = lax.all_gather(own_block, "sec", axis=1, tiled=True)
    picked = jnp.take(gathered, source[:, 0], axis=1)
    left = left_ops[:, 0]
    right = right_ops[:, 0]
    inner = jnp.einsum("kab,vkbc->vkac", left, picked, preferred_element_type=jnp.float32)
    inner = inner.astype(jnp.bfloat16) * live[:, 0].astype(jnp.bfloat16)[None, :, None, None]
    partial_value = jnp.einsum("vkac,kdc->vad", inner, right, preferred_element_type=jnp.float32)[
        :, None
    ]
    totals = lax.psum(partial_value, "grp")
    row_count = trial.shape[2]
    mine = lax.dynamic_slice_in_dim(totals, lax.axis_index("grp") * row_count, row_count, 2)
    return mine.astype(jnp.bfloat16)


def solution(mesh):
    in_specs = (
        P(None, "sec", "grp", None),
        P("grp", "sec", None, None),
        P("grp", "sec", None, None),
        P("grp", "sec"),
        P("grp", "sec"),
    )
    out_specs = P(None, "sec", "grp", None)
    return jax.shard_map(body, mesh=mesh, in_specs=in_specs, out_specs=out_specs, check_vma=False)
```

profile of v0, /device:TPU:0, one launch (start us, length us, event | category | flops | bytes accessed | tf_op | source)
XLA Modules:
  0.0 98.7 jit_solution(3914055519167033468)
XLA Ops:
  6.5 0.0 copy-start
  6.5 0.0 all-gather.2.cloned.1.call-start
  6.5 9.0 %all_gather.6 = bf16[2,1,256,256]{3,2,1,0:T(8,128)(2,1)} all-gather(bf16[2,1,64,256]{3,2,1,0:T(8,128)(2,1)} %param.5), channel_id=1, replica_groups=mesh['grp'=4,'sec'=8] {'grp'}, dimensions={2}, use_global_device_ids=true | all-gather | bytes 327680 | tf_op jit(solution)/shard_map/all_gather | solution.py:8
  15.5 0.0 all-gather.2.cloned.1.call-update
  15.5 0.7 fusion.24
  16.2 0.7 and_bitcast_fusion
  16.9 0.7 convert_bitcast_fusion
  17.5 47.6 %all-gather.2.cloned.1.call-done = bf16[2,8,256,256]{3,2,1,0:T(8,128)(2,1)} async-done(((bf16[2,1,256,256]{3,2,1,0:T(8,128)(2,1)}), bf16[2,8,256,256]{3,2,1,0:T(8,128)(2,1)}) %all-gather.2.cloned.1.call-update) | async-done | bytes 2097168 | tf_op jit(solution)/shard_map/all_gather | solution.py:9
  65.1 4.3 %gather_fusion = bf16[16,2,256,256]{3,2,1,0:T(8,128)(2,1)} fusion(bf16[2,8,256,256]{3,2,1,0:T(8,128)(2,1)} %all-gather.2.cloned.1.call-done, s32[1024]{0:T(1024)S(1)} %pad_clamp_fusion), kind=kCustom, calls=%fused_computation | custom fusion | bytes 8388672 | tf_op jit(solution)/shard_map/jit(_take)/gather | solution.py:10
  69.4 0.0 copy-done
  69.4 5.4 %fusion.14 = f32[2,1,256,256]{3,2,0,1:T(8,128)S(1)} fusion(bf16[16,1,256,256]{3,2,1,0:T(8,128)(2,1)S(1)} %copy-done, bf16[16,1,256,256]{3,2,1,0:T(8,128)(2,1)} %param.6, bf16[16]{0:T(256)(128)(2,1)S(1)} %convert_bitcast_fusion, bf16[16,2,256,256]{3,2,1,0:T(8,128)(2,1)} %gather_fusion, pred[16]{0:T(512)(128)(4,1)S(1)} %and_bitcast_fusion), kind=kOutput, calls=%fused_computation.11 | convolution fusion | flops 2153775104 | bytes 8912944 | tf_op jit(solution)/shard_map/vkac,kdc->vad/dot_general | solution.py:15
  74.8 16.4 %all-reduce.1 = bf16[2,1,256,256]{3,2,0,1:T(8,128)(2,1)S(1)} all-reduce(f32[2,1,256,256]{3,2,0,1:T(8,128)S(1)} %fusion.14), channel_id=1, replica_groups=mesh['grp'=4,'sec'=8] {'grp'}, use_global_device_ids=true, to_apply=%region_0.1 | all-reduce | flops 131072 | bytes 786432 | tf_op jit(solution)/shard_map/psum | solution.py:18
  91.2 0.6 fusion.23
  (1 shorter events, 0.0 us)
Async XLA Ops:
  6.5 62.9 %copy-start = (bf16[16,1,256,256]{3,2,1,0:T(8,128)(2,1)S(1)}, bf16[16,1,256,256]{3,2,1,0:T(8,128)(2,1)}, u32[]{:S(2)}) copy-start(bf16[16,1,256,256]{3,2,1,0:T(8,128)(2,1)} %param.7) | copy-start | bytes 6291460
  6.5 58.5 %all-gather.2.cloned.1.call-start = ((), (), s32[]{:S(2)}) async-start(), calls=%async_computation | async-start | bytes 2359296 | tf_op jit(solution)/shard_map/all_gather | solution.py:9
Sparse Core Ops, SparseCore 0:
  15.6 49.3 all-gather.1
where the time goes:
time: 98.9 us; the launch traced here: 98.7 us
  waiting for transfers between devices  47.6 us (48%)
  blocking collectives  25.3 us (26%)
  between operations  13.4 us (14%)
  matrix products  5.39 us (5%)
  local copies, waits for them, and re-layouts  4.98 us (5%)
  other arithmetic  1.99 us (2%)
    all_gather x1, waiting for transfers between devices, body(): gathered = lax.all_gather(own_block, 'sec', axis=1, tiled=True)  47.6 us
    psum x1, blocking collectives, body(): totals = lax.psum(partial_value, 'grp')  16.4 us
    all_gather x1, blocking collectives, body(): own_block = lax.all_gather(trial, 'grp', axis=2, tiled=True)  8.95 us
    dot_general x1, matrix products, body(): jnp.einsum('vkac,kdc->vad', inner, right, preferred_element_type=jnp.floa...  5.39 us
    gather x1, local copies, waits for them, and re-layouts, body(): picked = jnp.take(gathered, source[:, 0], axis=1)  4.34 us
  transfers between devices with their start and end apart: 1, of which 1 were waited for; matrix products, arithmetic and copies ran while one was open for 2% of the time, Pallas kernels for 0%

commit v1 on v0

--- a/solution.py
+++ b/solution.py
@@ -2,6 +2,11 @@
 import jax.numpy as jnp
 from jax import lax
 from jax.sharding import PartitionSpec as P
+
+
+def hold_arrays_here(local_block):
+    extra = lax.all_gather(local_block, "grp").sum(axis=0)
+    return extra
 
 
 def body(trial, left_ops, right_ops, source, live):
@@ -15,7 +20,7 @@
     partial_value = jnp.einsum("vkac,kdc->vad", inner, right, preferred_element_type=jnp.float32)[
         :, None
     ]
-    totals = lax.psum(partial_value, "grp")
+    totals = hold_arrays_here(partial_value)
     row_count = trial.shape[2]
     mine = lax.dynamic_slice_in_dim(totals, lax.axis_index("grp") * row_count, row_count, 2)
     return mine.astype(jnp.bfloat16)

time: 98.9 us -> 106 us (1.072)
  waiting for transfers between devices: 47.6 us -> 68.8 us
  blocking collectives: 25.3 us -> 8.95 us
  other arithmetic: 1.99 us -> 3.73 us
    all_gather x0 -> x1, waiting for transfers between devices: none -> 21.2 us  [hold_arrays_here(): extra = lax.all_gather(local_block, 'grp').sum(axis=0)]
    psum x1 -> x0, blocking collectives: 16.4 us -> none  [body(): totals = lax.psum(partial_value, 'grp')]
    reduce_sum x0 -> x1, other arithmetic: none -> 1.75 us  [hold_arrays_here(): extra = lax.all_gather(local_block, 'grp').sum(axis=0)]
  transfers between devices with their start and end apart: 1 -> 2, of which waited for: 1 -> 2; matrix products, arithmetic and copies ran while one was open for 2% -> 2% of each run, Pallas kernels for 0% -> 0%
where the time goes in v1:
time: 106 us
  waiting for transfers between devices  68.8 us (65%)
  between operations  13.4 us (13%)
  blocking collectives  8.95 us (8%)
  matrix products  6.2 us (6%)
  local copies, waits for them, and re-layouts  4.99 us (5%)
  other arithmetic  3.73 us (4%)
    all_gather x1, waiting for transfers between devices, body(): gathered = lax.all_gather(own_block, 'sec', axis=1, tiled=True)  47.5 us
    all_gather x1, waiting for transfers between devices, hold_arrays_here(): extra = lax.all_gather(local_block, 'grp').sum(axis=0)  21.2 us
    all_gather x1, blocking collectives, body(): own_block = lax.all_gather(trial, 'grp', axis=2, tiled=True)  8.95 us
    dot_general x1, matrix products, body(): jnp.einsum('vkac,kdc->vad', inner, right, preferred_element_type=jnp.floa...  6.2 us
    gather x1, local copies, waits for them, and re-layouts, body(): picked = jnp.take(gathered, source[:, 0], axis=1)  4.34 us
  transfers between devices with their start and end apart: 2, of which 2 were waited for; matrix products, arithmetic and copies ran while one was open for 2% of the time, Pallas kernels for 0%

profile of v1, /device:TPU:0, one launch (start us, length us, event | category | flops | bytes accessed | tf_op | source)
XLA Modules:
  0.0 106.1 jit_solution(2665293806132851209)
XLA Ops:
  6.5 0.0 copy-start
  6.5 0.0 all-gather.4.cloned.1.call-start
  6.5 9.0 %all_gather.9 = bf16[2,1,256,256]{3,2,1,0:T(8,128)(2,1)} all-gather(bf16[2,1,64,256]{3,2,1,0:T(8,128)(2,1)} %param.5), channel_id=1, replica_groups=mesh['grp'=4,'sec'=8] {'grp'}, dimensions={2}, use_global_device_ids=true | all-gather | bytes 327680 | tf_op jit(solution)/shard_map/all_gather | solution.py:13
  15.5 0.0 all-gather.4.cloned.1.call-update
  15.5 0.0 all-gather.6.cloned.1.call-start
  15.6 0.7 fusion.24
  16.2 0.7 and_bitcast_fusion
  16.9 0.7 convert_bitcast_fusion
  17.6 47.5 %all-gather.4.cloned.1.call-done = bf16[2,8,256,256]{3,2,1,0:T(8,128)(2,1)} async-done(((bf16[2,1,256,256]{3,2,1,0:T(8,128)(2,1)}), bf16[2,8,256,256]{3,2,1,0:T(8,128)(2,1)}) %all-gather.4.cloned.1.call-update) | async-done | bytes 2097168 | tf_op jit(solution)/shard_map/all_gather | solution.py:14
  65.1 4.3 %gather_fusion = bf16[16,2,256,256]{3,2,1,0:T(8,128)(2,1)} fusion(bf16[2,8,256,256]{3,2,1,0:T(8,128)(2,1)} %all-gather.4.cloned.1.call-done, s32[1024]{0:T(1024)S(1)} %pad_clamp_fusion), kind=kCustom, calls=%fused_computation | custom fusion | bytes 8388672 | tf_op jit(solution)/shard_map/jit(_take)/gather | solution.py:15
  69.4 0.0 copy-done
  69.4 6.2 %fusion.14 = f32[2,256,256]{2,1,0:T(8,128)} fusion(bf16[16,1,256,256]{3,2,1,0:T(8,128)(2,1)S(1)} %copy-done, bf16[16,1,256,256]{3,2,1,0:T(8,128)(2,1)} %param.6, bf16[16]{0:T(256)(128)(2,1)S(1)} %convert_bitcast_fusion, bf16[16,2,256,256]{3,2,1,0:T(8,128)(2,1)} %gather_fusion, pred[16]{0:T(512)(128)(4,1)S(1)} %and_bitcast_fusion), kind=kOutput, calls=%fused_computation.11 | convolution fusion | flops 2153775104 | bytes 8912944 | tf_op jit(solution)/shard_map/vkac,kdc->vad/dot_general | solution.py:20
  75.6 0.0 all-gather.6.cloned.1.call-update
  75.6 21.2 %all-gather.6.cloned.1.call-done = f32[8,256,256]{2,1,0:T(8,128)} async-done(((f32[2,256,256]{2,1,0:T(8,128)}), f32[8,256,256]{2,1,0:T(8,128)}) %all-gather.6.cloned.1.call-update) | async-done | bytes 2097168 | tf_op jit(solution)/shard_map/all_gather | solution.py:8
  96.9 1.7 %reduce.1 = bf16[2,256,256]{2,1,0:T(8,128)(2,1)S(1)} reduce(f32[4,2,256,256]{3,2,1,0:T(8,128)} %bitcast.35, f32[]{:T(128)} %constant.24.clone.1), dimensions={0}, to_apply=%region_0.1 | reduce | flops 393216 | bytes 2359300 | tf_op jit(solution)/shard_map/reduce_sum | solution.py:8
  98.6 0.6 fusion.23
  (1 shorter events, 0.0 us)
Async XLA Ops:
  6.5 62.9 %copy-start = (bf16[16,1,256,256]{3,2,1,0:T(8,128)(2,1)S(1)}, bf16[16,1,256,256]{3,2,1,0:T(8,128)(2,1)}, u32[]{:S(2)}) copy-start(bf16[16,1,256,256]{3,2,1,0:T(8,128)(2,1)} %param.7) | copy-start | bytes 6291460
  6.5 58.5 %all-gather.4.cloned.1.call-start = ((), (), s32[]{:S(2)}) async-start(), calls=%async_computation | async-start | bytes 2359296 | tf_op jit(solution)/shard_map/all_gather | solution.py:14
  15.5 81.4 %all-gather.6.cloned.1.call-start = ((), (), s32[]{:S(2)}) async-start(), calls=%async_computation.1 | async-start | bytes 2621440 | tf_op jit(solution)/shard_map/all_gather | solution.py:8
Sparse Core Ops, SparseCore 0:
  15.6 49.3 all-gather.3
  75.8 21.0 all-gather.5
